TPU v7x, 32 devices: a whole 2x2x4 slice. The times are simulated.
32 devices in a mesh: row: 4 (over y, core), col: 8 (over z, x).
Axes of the slice: x: 2, y: 2, z: 4, core: 2. Of those that a mesh axis runs over, the one named last changes fastest.
Arguments:
- old_vectors: float32 [8192, 4096], P('row', 'col'), may hold values from -6 to 6, as said below
- pole_values: float32 [8192], replicated, may hold values from 0 to 8192, as said below
- live_mask: int32 [8192], replicated, may hold values from 0 to 1, as said below
- position: int32 [8192], replicated, may hold values from 0 to 8191, as said below
- rank_weight: float32 [1], replicated, may hold values from 0.5 to 2
Outputs:
- new_vectors: float32 [8192, 8192], P('row', 'col')
Inputs may be any that keep to these rules, and one draw needn't show every extreme that they name: `pole_values`: strictly increasing; consecutive values differ by 0.2 or more. `old_vectors`: the entries of rows 4095 and 4096 have magnitude 0.5 to 1.5. Each merged position appears exactly once. In every aligned group of 16 consecutive columns s of the halves' eigenvectors (s = h * 4096 + m), exactly 12 have live_mask[position[s]] = 1.
All inputs are finite; a program needn't handle non-finite values.
Results may differ from a plain program's by a relative error of at most 0.0003.
Values sent between devices are 32-bit elements; how exact they have to be, the bound alone decides.
No kernel may reach another device: no remote copies, remote signals or barrier semaphores. Data moves between devices by JAX's collectives and lax.ppermute only.
A program may use at most 128 MiB of HBM per device.

v0:
```python
import jax
import jax.numpy as jnp
from jax import lax
from jax.sharding import PartitionSpec as P

BISECT = 40
DEFL_GROUP = 16
LIVE_GROUP = 12


def bracket_lengths(pole_values, live_mask, squares, rank_value):
    order_size = pole_values.shape[0]
    positions = jnp.arange(order_size, dtype=jnp.int32)
    marked = jnp.where(live_mask > 0, positions, order_size)
    shifted = jnp.concatenate([marked[1:], jnp.full((1,), order_size, jnp.int32)])
    following = lax.cummin(shifted, axis=0, reverse=True)
    weight_sum = rank_value * jnp.sum(squares)
    next_gap = pole_values[jnp.minimum(following, order_size - 1)] - pole_values
    return jnp.where(following < order_size, next_gap, weight_sum)


def bisect_roots(pole_here, bracket_len, pole_values, squares, live_mask, rank_value):
    pole_diff = pole_values[None, :] - pole_here[:, None]
    alive_cols = (live_mask > 0)[None, :]

    def halving(interval, unused):
        low_end, high_end = interval
        middle = 0.5 * (low_end + high_end)
        offset_gap = pole_diff - middle[:, None]
        summands = jnp.where(
            alive_cols, squares[None, :] / jnp.where(alive_cols, offset_gap, 1.0), 0.0
        )
        secular = 1.0 + rank_value * jnp.sum(summands, axis=1)
        is_below = secular < 0.0
        return ((jnp.where(is_below, middle, low_end), jnp.where(is_below, high_end, middle)), None)

    interval, unused = lax.scan(
        halving, (jnp.zeros_like(bracket_len), bracket_len), None, length=BISECT
    )
    return 0.5 * (interval[0] + interval[1])


def log_terms(pole_here, offsets, live_here, own_index, pole_values, live_mask):
    order_size = pole_values.shape[0]
    pole_diff = pole_values[None, :] - pole_here[:, None]
    on_pole = own_index[:, None] == jnp.arange(order_size, dtype=jnp.int32)[None, :]
    quotient = jnp.where(
        on_pole, offsets[:, None], 1.0 - offsets[:, None] / jnp.where(on_pole, 1.0, pole_diff)
    )
    in_play = (live_here[:, None] > 0) & (live_mask[None, :] > 0)
    logs = jnp.where(in_play, jnp.log(jnp.abs(jnp.where(in_play, quotient, 1.0))), 0.0)
    return jnp.sum(logs, axis=0)


def column_norms(pole_here, offsets, live_here, pole_values, live_mask, hat_weights):
    alive_cols = (live_mask > 0)[None, :]
    offset_gap = pole_values[None, :] - pole_here[:, None] - offsets[:, None]
    summands = jnp.where(
        alive_cols, hat_weights[None, :] ** 2 / jnp.where(alive_cols, offset_gap, 1.0) ** 2, 0.0
    )
    return jnp.where(live_here > 0, jnp.sqrt(jnp.sum(summands, axis=1)), 1.0)


def cauchy_tile(
    sorted_rows,
    pole_cols,
    offset_cols,
    norm_cols,
    live_cols,
    col_index,
    pole_values,
    live_mask,
    hat_weights,
):
    row_poles = pole_values[sorted_rows]
    row_hats = hat_weights[sorted_rows]
    row_live = live_mask[sorted_rows] > 0
    col_live = (live_cols > 0)[None, :]
    both_live = row_live[:, None] & col_live
    offset_gap = row_poles[:, None] - pole_cols[None, :] - offset_cols[None, :]
    entries = row_hats[:, None] / jnp.where(both_live, offset_gap, 1.0) / norm_cols[None, :]
    identity = (sorted_rows[:, None] == col_index[None, :]).astype(jnp.float32)
    return jnp.where(col_live, jnp.where(both_live, entries, 0.0), identity)


def hat_from(log_sum, coupling, live_mask, rank_value):
    return jnp.where(
        live_mask > 0, jnp.sign(coupling) * jnp.exp(0.5 * (log_sum - jnp.log(rank_value))), 0.0
    )


def shards(old_vectors, pole_values, live_mask, position, rank_weight):
    rank_value = rank_weight[0]
    order_size = pole_values.shape[0]
    half_order = order_size // 2
    rows_here = old_vectors.shape[0]
    cols_here = old_vectors.shape[1]
    row_count = lax.axis_size("row")
    col_count = lax.axis_size("col")
    row_rank = lax.axis_index("row")
    col_rank = lax.axis_index("col")
    upper_owner = (half_order - 1) // rows_here
    lower_owner = half_order // rows_here
    edge_rows = jnp.stack(
        [
            jnp.where(row_rank == upper_owner, old_vectors[(half_order - 1) % rows_here], 0.0),
            jnp.where(row_rank == lower_owner, old_vectors[half_order % rows_here], 0.0),
        ]
    )
    edge_rows = lax.psum(edge_rows, "row")
    edge_rows = lax.all_gather(edge_rows, "col", axis=1, tiled=True)
    boundary = jnp.concatenate([edge_rows[0], edge_rows[1]])
    spread = jnp.zeros((order_size,), jnp.float32).at[position].set(boundary)
    coupling = jnp.where(live_mask > 0, spread, 0.0)
    squares = coupling * coupling
    bracket_len = bracket_lengths(pole_values, live_mask, squares, rank_value)
    block_cols = order_size // col_count
    per_device = block_cols // row_count
    block_first = col_rank * block_cols
    own_first = block_first + row_rank * per_device
    block_index = block_first + jnp.arange(block_cols, dtype=jnp.int32)
    own_poles = lax.dynamic_slice_in_dim(pole_values, own_first, per_device)
    own_live = lax.dynamic_slice_in_dim(live_mask, own_first, per_device)
    own_bracket = lax.dynamic_slice_in_dim(bracket_len, own_first, per_device)
    block_poles = lax.dynamic_slice_in_dim(pole_values, block_first, block_cols)
    block_live = lax.dynamic_slice_in_dim(live_mask, block_first, block_cols)
    bisected = bisect_roots(own_poles, own_bracket, pole_values, squares, live_mask, rank_value)
    own_offsets = jnp.where(own_live > 0, bisected, 0.5 * own_bracket)
    block_offsets = lax.all_gather(own_offsets, "row", axis=0, tiled=True)
    grouped = (
        block_poles.reshape(row_count, per_device),
        block_offsets.reshape(row_count, per_device),
        block_live.reshape(row_count, per_device),
        block_index.reshape(row_count, per_device),
    )

    def log_group(members):
        return log_terms(members[0], members[1], members[2], members[3], pole_values, live_mask)

    partial_logs = jnp.sum(lax.map(log_group, grouped), axis=0)
    log_sum = lax.psum(partial_logs, "col")
    hat_weights = hat_from(log_sum, coupling, live_mask, rank_value)

    def norm_group(members):
        return column_norms(members[0], members[1], members[2], pole_values, live_mask, hat_weights)

    block_norms = lax.map(norm_group, (grouped[0], grouped[1], grouped[2])).reshape(block_cols)
    half_id = row_rank * rows_here // half_order
    half_base = half_id * half_order
    group_count = half_order // DEFL_GROUP
    column_live = jnp.take(live_mask, position)
    half_live = lax.dynamic_slice_in_dim(column_live, half_base, half_order).reshape(
        group_count, DEFL_GROUP
    )
    within = jnp.arange(DEFL_GROUP, dtype=jnp.int32)
    sort_keys = (1 - half_live) * DEFL_GROUP + within[None, :]
    group_order = jnp.argsort(sort_keys, axis=1)
    group_first = (jnp.arange(group_count, dtype=jnp.int32) * DEFL_GROUP)[:, None]
    live_list = (group_order[:, :LIVE_GROUP] + group_first).reshape(-1)
    dropped_list = (group_order[:, LIVE_GROUP:] + group_first).reshape(-1)
    live_count = cols_here // DEFL_GROUP * LIVE_GROUP
    dropped_count = cols_here - live_count
    column_first = col_rank * cols_here
    live_local = (
        lax.dynamic_slice_in_dim(live_list, col_rank * live_count, live_count) - column_first
    )
    dropped_local = (
        lax.dynamic_slice_in_dim(dropped_list, col_rank * dropped_count, dropped_count)
        - column_first
    )
    live_panel = jnp.take(old_vectors, live_local, axis=1)
    dropped_panel = jnp.take(old_vectors, dropped_local, axis=1)
    sorted_rows = jnp.take(position, half_base + live_list)
    cauchy = cauchy_tile(
        sorted_rows,
        block_poles,
        block_offsets,
        block_norms,
        block_live,
        block_index,
        pole_values,
        live_mask,
        hat_weights,
    )
    live_part = jnp.dot(
        lax.all_gather(live_panel, "col", axis=1, tiled=True),
        cauchy,
        precision=lax.Precision.HIGHEST,
        preferred_element_type=jnp.float32,
    )
    dropped_all = lax.all_gather(dropped_panel, "col", axis=1, tiled=True)
    inverse_map = (
        jnp.zeros((order_size,), jnp.int32)
        .at[position]
        .set(jnp.arange(order_size, dtype=jnp.int32))
    )
    source_index = lax.dynamic_slice_in_dim(inverse_map, block_first, block_cols)
    dropped_slot = (
        jnp.zeros((half_order,), jnp.int32)
        .at[dropped_list]
        .set(jnp.arange(dropped_list.shape[0], dtype=jnp.int32))
    )
    slot_here = jnp.take(dropped_slot, source_index % half_order)
    chosen = (block_live == 0) & (source_index // half_order == half_id)
    copied = jnp.take(dropped_all, slot_here, axis=1)
    new_vectors = live_part + jnp.where(chosen[None, :], copied, 0.0)
    return new_vectors


def solution(mesh):
    in_specs = (P("row", "col"), P(), P(), P(), P())
    out_specs = P("row", "col")
    return jax.shard_map(shards, mesh=mesh, in_specs=in_specs, out_specs=out_specs, check_vma=False)
```

profile of v0, /device:TPU:0, one launch (start us, length us, event | category | flops | bytes accessed | tf_op | source)
XLA Modules:
  0.0 766.7 jit_solution(15935491703908466170)
XLA Ops:
  7.3 45.5 %gather_fusion = s32[8192]{0:T(1024)S(1)} fusion(s32[8192]{0:T(1024)S(1)} %copy-done, s32[8192]{0:T(1024)S(1)} %get-tuple-element.291), kind=kCustom, calls=%fused_computation | custom fusion | bytes 98304 | tf_op jit(solution)/shard_map/jit(_take)/gather | solution.py:151
  54.2 5.3 copy.27
  64.7 6.5 gather_fusion.1
  74.0 8.5 %psum.14 = f32[2,512]{1,0:T(2,128)S(1)} all-reduce(f32[2,512]{1,0:T(2,128)S(1)} %pad_maximum_fusion.1), channel_id=1, replica_groups=mesh['row'=4,'col'=8] {'row'}, use_global_device_ids=true, to_apply=%region_1.2 | all-reduce | flops 1024 | bytes 8192 | tf_op jit(solution)/shard_map/psum | solution.py:110
  82.5 32.3 %all_gather.13 = f32[2,4096]{1,0:T(2,128)S(1)} all-gather(f32[2,512]{1,0:T(2,128)S(1)} %psum.14), channel_id=1, replica_groups=mesh['row'=4,'col'=8] {'col'}, dimensions={1}, use_global_device_ids=true | all-gather | bytes 36864 | tf_op jit(solution)/shard_map/all_gather | solution.py:111
  114.9 30.7 %scatter_custom_fusion = f32[8192]{0:T(1024)S(1)} fusion(s32[8192]{0:T(1024)S(1)} %get-tuple-element.290, f32[8192]{0:T(1024)S(1)} %pad_maximum_fusion, f32[]{:T(128)} %constant.222.clone.1), kind=kCustom, calls=%fused_computation.84 | custom fusion | bytes 32772 | tf_op jit(solution)/shard_map/scatter | solution.py:113
  150.9 45.5 %gather_fusion.4 = f32[8192]{0:T(1024)S(1)} fusion(f32[8192]{0:T(1024)S(1)} %copy-done.1, s32[8192]{0:T(1024)S(1)} %broadcast_clamp_fusion), kind=kCustom, calls=%fused_computation.4 | custom fusion | bytes 98304 | tf_op jit(solution)/shard_map/gather | solution.py:18
  196.6 142.5 %while.37 = (s32[]{:T(128)}, f32[256]{0:T(256)S(1)}, f32[256]{0:T(256)S(1)}, f32[]{:T(128)}, pred[1,8192]{1,0:T(4,128)(4,1)S(1)}, /*index=5*/f32[8192]{0:T(1024)...) while((s32[]{:T(128)}, f32[256]{0:T(256)S(1)}, ...), condition=%wide.region_8.9_spmd.clone, body=%wide.region_6.8_spmd.clone.sunk | while | flops 12584963 | bytes 102525 | solution.py:37
  339.4 17.4 %gather_fusion.2 = s32[3072]{0:T(1024)S(1)} fusion(s32[8192]{0:T(1024)S(1)} %copy-done.2, s32[3072]{0:T(1024)S(1)} %broadcast_clamp_fusion.2), kind=kCustom, calls=%fused_computation.2 | custom fusion | bytes 36864 | tf_op jit(solution)/shard_map/jit(_take)/gather | solution.py:173
  356.8 17.4 %gather_fusion.6 = f32[3072]{0:T(1024)S(1)} fusion(f32[8192]{0:T(1024)S(1)} %get-tuple-element.549, s32[3072]{0:T(1024)S(1)} %broadcast_clamp_fusion.3), kind=kCustom, calls=%fused_computation.6 | custom fusion | bytes 36864 | tf_op jit(solution)/shard_map/gather | solution.py:75
  374.3 17.4 %gather_fusion.3 = s32[3072]{0:T(1024)S(1)} fusion(s32[8192]{0:T(1024)S(1)} %copy-done, s32[3072]{0:T(1024)S(1)} %broadcast_clamp_fusion.3), kind=kCustom, calls=%fused_computation.3 | custom fusion | bytes 36864 | tf_op jit(solution)/shard_map/gather | solution.py:77
  391.9 30.5 %scatter_custom_fusion.1 = s32[8192]{0:T(1024)S(1)} fusion(s32[8192]{0:T(1024)S(1)} %get-tuple-element.290, s32[8192]{0:T(1024)S(1)} %iota.58, s32[]{:T(128)} %constant.162.clone.1), kind=kCustom, calls=%fused_computation.89 | custom fusion | bytes 32772 | tf_op jit(solution)/shard_map/scatter | solution.py:195
  422.5 5.1 all-gather
  427.6 21.9 %while.35 = (s32[]{:T(128)}, f32[4,8192]{1,0:T(4,128)S(1)}, s32[4,256]{1,0:T(4,128)S(1)}, s32[8192]{0:T(1024)S(1)}, s32[4,256]{1,0:T(4,128)S(1)}, /*index=5*/f32...) while((s32[]{:T(128)}, f32[4,8192]{1,0:T(4,128)S(1)}, ...), condition=%wide.region_11.12_spmd, body=%wide.region_9.11_spmd.sunk | while | flops 23068928 | bytes 191101 | solution.py:140
  427.6 4.9 fusion.59
  449.5 43.7 %psum.15 = f32[8192]{0:T(1024)S(1)} all-reduce(f32[8192]{0:T(1024)S(1)} %reduce_sum.48), channel_id=1, replica_groups=mesh['row'=4,'col'=8] {'col'}, use_global_device_ids=true, to_apply=%region_13.14 | all-reduce | flops 8192 | bytes 65536 | tf_op jit(solution)/shard_map/psum | solution.py:141
  493.3 17.4 %gather_fusion.5 = f32[3072]{0:T(1024)S(1)} fusion(f32[8192]{0:T(1024)S(1)} %get-tuple-element.270, s32[3072]{0:T(1024)S(1)} %broadcast_clamp_fusion.3), kind=kCustom, calls=%fused_computation.5 | custom fusion | bytes 36864 | tf_op jit(solution)/shard_map/gather | solution.py:76
  510.7 12.9 %while.36 = (s32[]{:T(128)}, f32[4,256]{1,0:T(4,128)S(1)}, s32[4,256]{1,0:T(4,128)S(1)}, s32[8192]{0:T(1024)S(1)}, f32[1,8192]{1,0:T(1,128)S(1)}, /*index=5*/f32...) while((s32[]{:T(128)}, f32[4,256]{1,0:T(4,128)S(1)}, ...), condition=%wide.region_16.17_spmd, body=%wide.region_14.16_spmd.sunk | while | flops 14688514 | bytes 129145 | solution.py:147
  528.0 6.2 gather_fusion.7
  534.3 9.8 %fusion.54 = f32[3072,1024]{1,0:T(8,128)} fusion(s32[1024]{0:T(1024)S(1)} %iota_add_fusion.1, f32[1024]{0:T(1024)S(1)} %bitcast.80, f32[1024]{0:T(1024)S(1)} %bitcast.76, f32[1024]{0:T(1024)S(1)} %dynamic_slice.62, f32[3072]{0:T(1024)S(1)} %gather_fusion.6, f32[3072]{0:T(1024)S(1)} %gather_fusion.5, s32[3072]{0:T(1024)S(1)} %and_select_fusion.5, ...), kind=kLoop, calls=%fused_computation.44.clone.clone.clone.clone.1 | loop fusion | flops 31457280 | bytes 12640256 | tf_op jit(solution)/shard_map/dot_general | solution.py:185
  544.1 12.2 %gather_fusion.9 = f32[1024,2048]{1,0:T(8,128)} fusion(f32[2048,1024]{0,1:T(8,128)} %all-gather.6.cloned.1.call-done, s32[1024]{0:T(1024)S(1)} %broadcast_clamp_fusion.4), kind=kCustom, calls=%fused_computation.9 | custom fusion | bytes 16781312 | tf_op jit(solution)/shard_map/jit(_take)/gather | solution.py:205
  556.4 9.2 %copy.32 = f32[1024,2048]{0,1:T(8,128)} copy(f32[1024,2048]{1,0:T(8,128)} %gather_fusion.9) | data formatting | bytes 16777216 | tf_op jit(solution)/shard_map/jit(_take)/gather | solution.py:205
  565.6 107.8 %all-gather.4.cloned.1.call-done = f32[2048,3072]{0,1:T(8,128)} async-done(((f32[2048,384]{0,1:T(8,128)}), f32[2048,3072]{0,1:T(8,128)}) %all-gather.4.cloned.1.call-update) | async-done | bytes 25165840 | tf_op jit(solution)/shard_map/all_gather | solution.py:186
  673.4 86.5 %bitcast_add_fusion = f32[2048,1024]{1,0:T(8,128)} fusion(f32[1024,2048]{0,1:T(8,128)} %copy.32, f32[2048,3072]{0,1:T(8,128)} %all-gather.4.cloned.1.call-done, pred[1024]{0:T(1024)(128)(4,1)S(1)} %get-tuple-element.264, pred[1024]{0:T(1024)(128)(4,1)S(1)} %get-tuple-element.292, f32[3072,1024]{1,0:T(8,128)} %fusion.54), kind=kOutput, calls=%fused_computation.50 | convolution fusion | flops 77315702784 | bytes 54528000 | tf_op jit(solution)/shard_map/dot_general | solution.py:185
  (286 shorter events, 190.1 us)
Async XLA Ops:
  6.5 0.8 copy-start
  6.5 537.6 %all-gather.6.cloned.1.call-start = ((), (), s32[]{:S(2)}) async-start(), calls=%async_computation.1 | async-start | bytes 9437184 | tf_op jit(solution)/shard_map/all_gather | solution.py:191
  64.3 609.0 %all-gather.4.cloned.1.call-start = ((), (), s32[]{:S(2)}) async-start(), calls=%async_computation | async-start | bytes 28311552 | tf_op jit(solution)/shard_map/all_gather | solution.py:186
  71.3 79.6 %copy-start.1 = (f32[8192]{0:T(1024)S(1)}, f32[8192]{0:T(1024)}, u32[]{:S(2)}) copy-start(f32[8192]{0:T(1024)} %param.12) | copy-start | bytes 98308
  196.5 142.9 %copy-start.2 = (s32[8192]{0:T(1024)S(1)}, s32[8192]{0:T(1024)}, u32[]{:S(2)}) copy-start(s32[8192]{0:T(1024)} %param.14) | copy-start | bytes 98308
Sparse Core Ops, SparseCore 0:
  64.5 127.4 all-gather.5
  193.5 479.7 all-gather.3
where the time goes:
time: 768 us; the launch traced here: 767 us
  local copies, waits for them, and re-layouts  273 us (36%)
  other arithmetic  193 us (25%)
  waiting for transfers between devices  108 us (14%)
  blocking collectives  89.6 us (12%)
  matrix products  86.5 us (11%)
  between operations  15.2 us (2%)
    reduce_sum x40, other arithmetic, halving(): secular = 1.0 + rank_value * jnp.sum(summands, axis=1)  111 us
    all_gather x1, waiting for transfers between devices, shards(): lax.all_gather(live_panel, 'col', axis=1, tiled=True)  108 us
    dot_general x1, matrix products, shards(): jnp.dot(lax.all_gather(live_panel, 'col', axis=1, tiled=True), cauchy, pr...  86.5 us
    gather x1, local copies, waits for them, and re-layouts, shards(): column_live = jnp.take(live_mask, position)  45.5 us
    gather x1, local copies, waits for them, and re-layouts, bracket_lengths(): next_gap = pole_values[jnp.minimum(following, order_size - 1)] - pole_values  45.5 us
    psum x1, blocking collectives, shards(): log_sum = lax.psum(partial_logs, 'col')  43.7 us
    all_gather x1, blocking collectives, shards(): edge_rows = lax.all_gather(edge_rows, 'col', axis=1, tiled=True)  32.3 us
    scatter x1, local copies, waits for them, and re-layouts, shards(): spread = jnp.zeros((order_size,), jnp.float32).at[position].set(boundary)  30.7 us
  transfers between devices with their start and end apart: 2, of which 1 were waited for; matrix products, arithmetic and copies ran while one was open for 53% of the time, Pallas kernels for 0%

commit v1 on v0

v1 whole, which is shorter than its diff:
```python
import functools

import jax
import jax.numpy as jnp
from jax import lax
from jax.experimental import pallas as pl
from jax.experimental.pallas import tpu as pltpu
from jax.sharding import PartitionSpec as P


FAR = 1e30
FIRST = (4, 5, 6)
LANES = 128
F32 = jnp.float32
BF16 = jnp.bfloat16
VMEM = pltpu.VMEM


def whole(shape):
    return pl.BlockSpec(shape, lambda *_: (0,) * len(shape))


def lookup_kernel(slot_ref, table_ref, mask_ref, pole_ref, live_ref):
    count = slot_ref.shape[1]
    width = min(1024, count)
    table = table_ref[...]
    top = table.astype(BF16)
    rest = table - top.astype(F32)
    middle = rest.astype(BF16)
    low = (rest - middle.astype(F32)).astype(BF16)
    stacked = jnp.concatenate([top, middle, low, mask_ref[...].astype(BF16)], axis=0)
    rows = table.shape[1]
    for first in range(0, count, width):
        slot = slot_ref[:, first : first + width]
        chosen = lax.broadcasted_iota(jnp.int32, (rows, width), 0) == (slot >> 7)
        picked = jnp.dot(
            stacked, jnp.where(chosen, 1.0, 0.0).astype(BF16), preferred_element_type=F32
        )
        on_lane = lax.broadcasted_iota(jnp.int32, (LANES, width), 0) == (slot & (LANES - 1))
        value = (picked[:LANES] + picked[LANES : 2 * LANES]) + picked[2 * LANES : 3 * LANES]
        pole_ref[:, first : first + width] = jnp.sum(
            jnp.where(on_lane, value, 0.0), axis=0, keepdims=True
        )
        live_ref[:, first : first + width] = jnp.sum(
            jnp.where(on_lane, picked[3 * LANES :], 0.0), axis=0, keepdims=True
        )


def root_kernel(
    rank_ref, pole_ref, live_ref, edge_ref, own_ref, own_live_ref, root_ref, square, far, delta
):
    alive = live_ref[...] > 0.5
    square[...] = jnp.where(alive, edge_ref[...] * edge_ref[...], 0.0) * rank_ref[0]
    far[...] = jnp.where(alive, pole_ref[...], FAR)
    total = jnp.sum(square[...], axis=1, keepdims=True)
    count = own_ref.shape[0]
    tile = delta.shape[0]
    span = delta.shape[1]
    unroll = 8
    steps = span // (LANES * unroll)

    def spread(column):
        return jnp.broadcast_to(column, (tile, LANES))

    def one_tile(number, carry):
        rows = pl.ds(pl.multiple_of(number * tile, tile), tile)
        here = spread(own_ref[rows, :])

        def prepare(step, sums):
            gap, weight = sums
            for part in range(unroll):
                lanes = pl.ds(pl.multiple_of((step * unroll + part) * LANES, LANES), LANES)
                apart = far[:, lanes] - here
                gap = jnp.minimum(gap, jnp.where(apart > 0.0, apart, FAR))
                at_own = apart == 0.0
                weight = weight + jnp.where(at_own, square[:, lanes], 0.0)
                delta[:, lanes] = jnp.where(at_own, FAR, apart)
            return gap, weight

        zero = jnp.zeros((tile, LANES), F32)
        gap, weight = lax.fori_loop(0, steps, prepare, (zero + FAR, zero))
        gap = jnp.min(gap, axis=1, keepdims=True)
        weight = jnp.sum(weight, axis=1, keepdims=True)
        is_last = gap > 0.1 * FAR
        length = jnp.where(is_last, jnp.broadcast_to(total, gap.shape), gap)
        own_live = own_live_ref[rows, :] > 0

        def improve(state):
            turn, _, low, high, point = state
            shift = spread(point)

            def gather(step, sums):
                value, slope = sums
                for part in range(unroll):
                    lanes = pl.ds(pl.multiple_of((step * unroll + part) * LANES, LANES), LANES)
                    inverse = 1.0 / (delta[:, lanes] - shift)
                    term = square[:, lanes] * inverse
                    value = value + term
                    slope = slope + term * inverse
                return value, slope

            value, slope = lax.fori_loop(0, steps, gather, (zero, zero))
            value = 1.0 + jnp.sum(value, axis=1, keepdims=True)
            slope = jnp.sum(slope, axis=1, keepdims=True)
            is_below = value - weight / point < 0.0
            low = jnp.where(is_below, point, low)
            high = jnp.where(is_below, high, point)
            ahead = length - point
            near = jnp.where(is_last, weight + slope * point * point, weight)
            other = jnp.where(is_last, 0.0, slope * ahead * ahead)
            constant = jnp.where(is_last, value + slope * point, value - slope * ahead)
            middle = constant * length + near + other
            lean = constant * length - near + other
            spread_root = jnp.sqrt(lean * lean + 4.0 * near * other)
            rising = middle > 0.0
            target = jnp.where(
                rising,
                2.0 * near * length / jnp.where(rising, middle + spread_root, 1.0),
                (middle - spread_root) / jnp.where(rising, 1.0, 2.0 * constant),
            )
            change = jnp.abs(target - point)
            fits = ((target >= low) & (target <= high)) | (change <= 1e-5 * point)
            target = jnp.where(fits, target, 0.5 * (low + high))
            change = jnp.abs(target - point)
            still = jnp.where(own_live & (change > 4e-6 * target), 1.0, 0.0)
            return turn + 1, jnp.max(still), low, high, target

        start = 0.5 * length
        state = (jnp.int32(0), jnp.float32(1.0), jnp.zeros_like(length), length, start)
        state = lax.while_loop(lambda s: (s[0] < 48) & (s[1] > 0.5), improve, state)
        root_ref[rows, :] = jnp.where(own_live, state[4], 0.5 * length)
        return carry

    lax.fori_loop(0, count // tile, one_tile, 0)


def log_kernel(pole_ref, column_ref, sum_ref):
    count = pole_ref.shape[1]
    width = min(512, count)
    depth = column_ref.shape[0]
    group = 4
    for first in range(0, count, width):
        here = pole_ref[:, first : first + width]

        def body(step, total):
            product = None
            for part in range(group):
                rows = pl.ds(pl.multiple_of((step * group + part) * 8, 8), 8)
                offset = column_ref[rows, 1:2]
                apart = here - column_ref[rows, 0:1]
                ratio = jnp.where(apart == 0.0, offset, 1.0 - offset / apart)
                product = ratio if product is None else product * ratio
            return total + jnp.log(jnp.abs(product))

        total = lax.fori_loop(
            0, depth // (8 * group), body, jnp.zeros((8, width), F32), unroll=2
        )
        sum_ref[:, first : first + width] = jnp.sum(total, axis=0, keepdims=True)


def norm_kernel(far_ref, hat_ref, column_ref, norm_ref):
    count = column_ref.shape[0]
    span = far_ref.shape[1]
    tile = min(32, count)
    unroll = 8

    def one_tile(number, carry):
        rows = pl.ds(pl.multiple_of(number * tile, tile), tile)
        here = jnp.broadcast_to(column_ref[rows, 0:1], (tile, LANES))
        offset = jnp.broadcast_to(column_ref[rows, 1:2], (tile, LANES))

        def body(step, total):
            for part in range(unroll):
                lanes = pl.ds(pl.multiple_of((step * unroll + part) * LANES, LANES), LANES)
                entry = hat_ref[:, lanes] / ((far_ref[:, lanes] - here) - offset)
                total = total + entry * entry
            return total

        total = lax.fori_loop(0, span // (LANES * unroll), body, jnp.zeros((tile, LANES), F32))
        norm = jnp.sqrt(jnp.sum(total, axis=1, keepdims=True))
        norm_ref[rows, :] = jnp.where(column_ref[rows, 2:3] > 0.5, norm, 1.0)
        return carry

    lax.fori_loop(0, count // tile, one_tile, 0)


def cauchy_kernel(place_ref, column_ref, row_ref, high_ref, low_ref):
    depth, _ = high_ref.shape
    strip = 16
    pole_cols = row_ref[0:1, :]
    offset_cols = row_ref[1:2, :]
    dropped_cols = row_ref[2:3, :]
    live_cols = row_ref[3:4, :]

    def body(step, carry):
        rows = pl.ds(pl.multiple_of(step * strip, strip), strip)
        gap = (column_ref[rows, 0:1] - pole_cols) - offset_cols
        entry = (column_ref[rows, 2:3] / gap) * live_cols
        entry = jnp.where(column_ref[rows, 1:2] == dropped_cols, 1.0, entry)
        high = entry.astype(BF16)
        high_ref[rows, :] = high
        low_ref[rows, :] = (entry - high.astype(F32)).astype(BF16)
        return carry

    lax.fori_loop(0, depth // strip, body, 0, unroll=4)


def product_kernel(pieces, place_ref, *refs):
    piece_refs = refs[:pieces]
    weight_ref, high_ref, low_ref, out_ref, split = refs[pieces:]
    rows, depth = piece_refs[0].shape

    @pl.when(pl.program_id(0) == 0)
    def _():
        for number in range(pieces):
            value = piece_refs[number][...] * weight_ref[pl.ds(place_ref[number], 1), :]
            high = value.astype(BF16)
            lanes = slice(number * depth, (number + 1) * depth)
            split[:rows, lanes] = high
            split[rows:, lanes] = (value - high.astype(F32)).astype(BF16)

    both = jnp.dot(split[...], high_ref[...], preferred_element_type=F32)
    cross = jnp.dot(split[:rows, :], low_ref[...], preferred_element_type=F32)
    out_ref[...] = both[:rows] + (both[rows:] + cross)


def xor_permute(value, bit, count):
    return lax.ppermute(value, "col", [(source, source ^ bit) for source in range(count)])


def xor_gather(value, count, limit, axis):
    rank = lax.axis_index("col")
    bit = 1
    while bit < limit:
        other = xor_permute(value, bit, count)
        after = (rank & bit) > 0
        value = jnp.concatenate(
            [jnp.where(after, other, value), jnp.where(after, value, other)], axis=axis
        )
        bit *= 2
    return value


def shards(old_vectors, pole_values, live_mask, position, rank_weight):
    order_size = pole_values.shape[0]
    half_order = order_size // 2
    rows_here, cols_here = old_vectors.shape
    row_count = lax.axis_size("row")
    col_count = lax.axis_size("col")
    row_rank = lax.axis_index("row")
    col_rank = lax.axis_index("col")
    group = min(4, col_count)
    block_cols = order_size // col_count
    per_device = block_cols // row_count
    quarter = rows_here // group
    cut = quarter // 2
    chunks = ((0, cut), (cut, quarter - cut))
    member = col_rank % group
    half_id = row_rank * rows_here // half_order
    half_base = half_id * half_order

    table_rows = order_size // LANES
    pole_list, live_list = pl.pallas_call(
        lookup_kernel,
        out_shape=[jax.ShapeDtypeStruct((1, order_size), F32)] * 2,
        name="lookup",
    )(
        position[None, :],
        pole_values.reshape(table_rows, LANES).T,
        live_mask.astype(F32).reshape(table_rows, LANES).T,
    )

    upper_owner = (half_order - 1) // rows_here
    lower_owner = half_order // rows_here
    edge = jnp.stack(
        [
            jnp.where(row_rank == upper_owner, old_vectors[(half_order - 1) % rows_here], 0.0),
            jnp.where(row_rank == lower_owner, old_vectors[half_order % rows_here], 0.0),
        ]
    )
    edge = lax.psum(edge, "row")
    edge = xor_gather(edge, col_count, col_count, 1).reshape(1, order_size)

    def send(chunk, bit, token):
        first, count = chunks[chunk]
        target = (member ^ (bit % group)) * quarter + first
        part = lax.dynamic_slice_in_dim(old_vectors, target, count, 0)
        if not bit:
            return part
        if token is not None:
            part, _ = lax.optimization_barrier((part, token))
        return xor_permute(part, bit, col_count)

    pieces = [{}, {}]
    for number, bit in enumerate(FIRST):
        if bit < col_count:
            pieces[0][bit] = send(0, bit, None if number == 0 else edge)

    block_first = col_rank * block_cols
    own_first = block_first + row_rank * per_device
    own_poles = lax.dynamic_slice_in_dim(pole_values, own_first, per_device)[:, None]
    own_live = lax.dynamic_slice_in_dim(live_mask, own_first, per_device)[:, None]
    tile = min(32, per_device)
    in_vmem = pl.BlockSpec(memory_space=VMEM)
    solve = pl.pallas_call(
        root_kernel,
        out_shape=jax.ShapeDtypeStruct((per_device, 1), F32),
        in_specs=[pl.BlockSpec(memory_space=pltpu.SMEM)] + [in_vmem] * 5,
        out_specs=in_vmem,
        scratch_shapes=[
            VMEM((1, order_size), F32),
            VMEM((1, order_size), F32),
            VMEM((tile, order_size), F32),
        ],
        name="roots",
    )
    own_offsets = solve(rank_weight, pole_list, live_list, edge, own_poles, own_live)

    block_offsets = lax.all_gather(own_offsets[:, 0], "row", axis=0, tiled=True)
    block_poles = lax.dynamic_slice_in_dim(pole_values, block_first, block_cols)
    block_live = lax.dynamic_slice_in_dim(live_mask, block_first, block_cols) > 0

    group_offsets = xor_gather(block_offsets[None, :], col_count, group, 1)

    range_cols = order_size // row_count
    range_first = row_rank * range_cols
    range_poles = lax.dynamic_slice_in_dim(pole_list, range_first, range_cols, 1)
    log_sum = pl.pallas_call(
        log_kernel,
        out_shape=jax.ShapeDtypeStruct((1, range_cols), F32),
        name="logs",
    )(
        range_poles,
        jnp.stack([block_poles, jnp.where(block_live, block_offsets, 0.0)], axis=1),
    )
    bit = 1
    while bit < col_count:
        log_sum = log_sum + xor_permute(log_sum, bit, col_count)
        bit *= 2

    def send_rest(chunk, token):
        for bit in list(range(group, col_count)) + list(range(group)):
            if bit not in pieces[chunk]:
                pieces[chunk][bit] = send(chunk, bit, token)

    send_rest(0, (log_sum, group_offsets))
    range_edge = lax.dynamic_slice_in_dim(edge, range_first, range_cols, 1)
    range_live = lax.dynamic_slice_in_dim(live_list, range_first, range_cols, 1) > 0.5
    hats = jnp.where(
        range_live,
        jnp.sign(range_edge) * jnp.exp(0.5 * (log_sum - jnp.log(rank_weight[0]))),
        0.0,
    )
    hats = lax.all_gather(hats, "row", axis=1, tiled=True)
    send_rest(1, hats)
    far_list = jnp.where(live_list > 0.5, pole_list, FAR)

    group_first = (col_rank // group) * group * block_cols
    group_cols = group * block_cols
    group_poles = lax.dynamic_slice_in_dim(pole_values, group_first, group_cols)[None, :]
    group_live = lax.dynamic_slice_in_dim(live_mask, group_first, group_cols)[None, :] > 0
    row_table = jnp.concatenate(
        [
            jnp.where(group_live, group_poles, -FAR),
            group_offsets,
            jnp.where(group_live, -2.0, group_poles),
            group_live.astype(F32),
        ],
        axis=0,
    )
    half_poles = lax.dynamic_slice_in_dim(pole_list[0], half_base, half_order)
    half_live = lax.dynamic_slice_in_dim(live_list[0], half_base, half_order) > 0.5
    column_table = jnp.stack(
        [
            jnp.where(half_live, half_poles, FAR),
            jnp.where(half_live, -1.0, half_poles),
            half_live.astype(F32),
        ],
        axis=1,
    )
    half_hats = lax.dynamic_slice_in_dim(hats[0], half_base, half_order)
    weights = jnp.where(half_live, half_hats, 1.0).reshape(col_count, cols_here)
    row_table, _ = lax.optimization_barrier((row_table, log_sum))
    sources = jnp.bitwise_xor(col_rank, jnp.arange(col_count, dtype=jnp.int32)).astype(jnp.int32)
    wide = min(1024, block_cols)
    tiles = block_cols // wide

    def cauchy(bit):
        place = jnp.concatenate([sources, (member ^ bit)[None].astype(jnp.int32)])
        grid_spec = pltpu.PrefetchScalarGridSpec(
            num_scalar_prefetch=1,
            grid=(col_count, tiles),
            in_specs=[
                pl.BlockSpec((cols_here, 3), lambda i, j, place: (place[i], 0)),
                pl.BlockSpec((4, wide), lambda i, j, place: (0, place[col_count] * tiles + j)),
            ],
            out_specs=[pl.BlockSpec((cols_here, wide), lambda i, j, place: (i, j))] * 2,
        )
        return pl.pallas_call(
            cauchy_kernel,
            out_shape=[jax.ShapeDtypeStruct((half_order, block_cols), BF16)] * 2,
            grid_spec=grid_spec,
            cost_estimate=pl.CostEstimate(
                flops=20 * half_order * block_cols,
                bytes_accessed=4 * half_order * block_cols,
                transcendentals=half_order * block_cols,
            ),
            name="cauchy",
        )(place, column_table, row_table)

    tile_cols = min(256, block_cols)

    def product(parts, high, low):
        rows = parts[0].shape[0]
        grid_spec = pltpu.PrefetchScalarGridSpec(
            num_scalar_prefetch=1,
            grid=(block_cols // tile_cols,),
            in_specs=[whole((rows, cols_here))] * col_count
            + [whole((col_count, cols_here))]
            + [pl.BlockSpec((half_order, tile_cols), lambda i, place: (0, i))] * 2,
            out_specs=pl.BlockSpec((rows, tile_cols), lambda i, place: (0, i)),
            scratch_shapes=[VMEM((2 * rows, half_order), BF16)],
        )
        return pl.pallas_call(
            functools.partial(product_kernel, col_count),
            out_shape=jax.ShapeDtypeStruct((rows, block_cols), F32),
            grid_spec=grid_spec,
            cost_estimate=pl.CostEstimate(
                flops=6 * rows * half_order * block_cols,
                bytes_accessed=4 * half_order * block_cols,
                transcendentals=0,
            ),
            name="product",
        )(sources, *parts, weights, high, low)

    order = list(range(group - 1, -1, -1))
    cauchys = {}
    for bit in order:
        cauchys[bit] = cauchy(bit)
    blocks = []
    for chunk in range(2):
        parts = [pieces[chunk][bit] for bit in range(col_count)]
        done = {}
        for bit in order:
            done[bit] = product(parts, *cauchys[bit])
        for bit in order[-1:] + order[:-1]:
            block = xor_permute(done[bit], bit, col_count) if bit else done[bit]
            blocks.append((block, (member ^ bit) * quarter + chunks[chunk][0]))
    norm_hats, _ = lax.optimization_barrier((hats, done[order[-2]]))
    measure = pl.pallas_call(
        norm_kernel,
        out_shape=jax.ShapeDtypeStruct((per_device, 1), F32),
        name="norms",
    )
    norms = measure(
        far_list,
        norm_hats,
        jnp.concatenate([own_poles, own_offsets, own_live.astype(F32)], axis=1),
    )
    block_norms = lax.all_gather(norms[:, 0], "row", axis=0, tiled=True)[None, :]
    new_vectors = jnp.zeros((rows_here, block_cols), F32)
    for block, first in blocks:
        new_vectors = lax.dynamic_update_slice_in_dim(new_vectors, block / block_norms, first, 0)
    return new_vectors


def solution(mesh):
    in_specs = (P("row", "col"), P(), P(), P(), P())
    out_specs = P("row", "col")
    return jax.shard_map(shards, mesh=mesh, in_specs=in_specs, out_specs=out_specs, check_vma=False)
```

time: 768 us -> 449 us (0.58)
  local copies, waits for them, and re-layouts: 273 us -> 17.4 us
  Pallas kernels: 0 us -> 205 us
  other arithmetic: 193 us -> 22.8 us
  matrix products: 86.5 us -> 0 us
  blocking collectives: 89.6 us -> 28.3 us
  starting transfers between devices: 0.04 us -> 43.1 us
  waiting for transfers between devices: 108 us -> 131 us
  between operations: 15.2 us -> 0.94 us
    pallas_call x0 -> x16, Pallas kernels: none -> 205 us  [the longest x8 108 us: product(): pl.pallas_call(functools.partial(product_kernel, col_count), out_shape=ja...]
    gather x11 -> x0, local copies, waits for them, and re-layouts: 198 us -> none  [the longest x1 45.5 us: shards(): column_live = jnp.take(live_mask, position)]
    reduce_sum x50 -> x0, other arithmetic: 144 us -> none  [the longest x40 111 us: halving(): secular = 1.0 + rank_value * jnp.sum(summands, axis=1)]
    ppermute x0 -> x28, waiting for transfers between devices: none -> 131 us  [xor_permute(): lax.ppermute(value, 'col', [(source, source ^ bit) for source in range(co...]
    all_gather x2 -> x0, waiting for transfers between devices: 108 us -> none  [the longest x1 108 us: shards(): lax.all_gather(live_panel, 'col', axis=1, tiled=True)]
    dot_general x1 -> x0, matrix products: 86.5 us -> none  [shards(): jnp.dot(lax.all_gather(live_panel, 'col', axis=1, tiled=True), cauchy, pr...]
    scatter x3 -> x0, local copies, waits for them, and re-layouts: 65.5 us -> none  [the longest x1 30.7 us: shards(): spread = jnp.zeros((order_size,), jnp.float32).at[position].set(boundary)]
    psum x2 -> x1, blocking collectives: 52.3 us -> 8.4 us  [shards(): edge = lax.psum(edge, 'row')]
  transfers between devices with their start and end apart: 2 -> 28, of which waited for: 1 -> 10; matrix products, arithmetic and copies ran while one was open for 53% -> 8% of each run, Pallas kernels for 0% -> 46%
where the time goes in v1:
time: 449 us; the launch traced here: 448 us
  Pallas kernels  205 us (46%)
  waiting for transfers between devices  131 us (29%)
  starting transfers between devices  43.1 us (10%)
  blocking collectives  28.3 us (6%)
  other arithmetic  22.8 us (5%)
  local copies, waits for them, and re-layouts  17.4 us (4%)
    ppermute x28, waiting for transfers between devices, xor_permute(): lax.ppermute(value, 'col', [(source, source ^ bit) for source in range(co...  131 us
    pallas_call x8, Pallas kernels, product(): pl.pallas_call(functools.partial(product_kernel, col_count), out_shape=ja...  108 us
    pallas_call x4, Pallas kernels, cauchy(): pl.pallas_call(cauchy_kernel, out_shape=[jax.ShapeDtypeStruct((half_order...  54.4 us
    ppermute x28, starting transfers between devices, xor_permute(): lax.ppermute(value, 'col', [(source, source ^ bit) for source in range(co...  43.1 us
    pallas_call x1, Pallas kernels, shards(): solve(rank_weight, pole_list, live_list, edge, own_poles, own_live)  24.1 us
    dynamic_update_slice x8, other arithmetic, shards(): lax.dynamic_update_slice_in_dim(new_vectors, block / block_norms, first, 0)  13.8 us
  transfers between devices with their start and end apart: 28, of which 10 were waited for; matrix products, arithmetic and copies ran while one was open for 8% of the time, Pallas kernels for 46%

profile of v1, /device:TPU:0, one launch (start us, length us, event | category | flops | bytes accessed | tf_op | source)
XLA Modules:
  0.0 448.4 jit_solution(13591071771528995553)
XLA Ops:
  0.8 8.4 %psum.7 = f32[2,512]{1,0:T(2,128)S(1)} all-reduce(f32[2,512]{1,0:T(2,128)S(1)} %pad_maximum_fusion.8), channel_id=1, replica_groups=mesh['row'=4,'col'=8] {'row'}, use_global_device_ids=true, to_apply=%region_0.1 | all-reduce | flops 1024 | bytes 8192 | tf_op jit(solution)/shard_map/psum | solution.py:281
  40.4 24.1 %roots.1 = f32[256,1]{1,0:T(8,128)} custom-call(f32[1]{0:T(128)S(6)} %copy.48.rank_ref, f32[1,8192]{1,0:T(1,128)} %get-tuple-element.26.pole_ref, f32[1,8192]{1,0:T(1,128)} %get-tuple-element.27.live_ref, f32[1,8192]{1,0:T(1,128)} %bitcast.32, f32[256,1]{1,0:T(8,128)} %copy.30.own_ref, s32[256,1]{1,0:T(8,128)} %copy.31.own_live_ref), custom_call_target="tpu_custom_call" | custom-call | tf_op jit(solution)/shard_map/roots/pallas_call | solution.py:317
  64.4 8.0 %all-gather = f32[1024,1]{1,0:T(8,128)S(1)} all-gather(f32[256,1]{1,0:T(8,128)} %roots.1), channel_id=2, replica_groups=mesh['row'=4,'col'=8] {'row'}, dimensions={0}, use_global_device_ids=true | all-gather | bytes 5120 | tf_op jit(solution)/shard_map/all_gather | solution.py:319
  75.1 8.8 %logs.1 = f32[1,2048]{1,0:T(1,128)} custom-call(f32[1,2048]{1,0:T(1,128)} %constant_dynamic-slice_fusion.6.pole_ref, f32[1024,2]{1,0:T(8,128)} %copy.32.column_ref), custom_call_target="tpu_custom_call" | custom-call | tf_op jit(solution)/shard_map/logs/pallas_call | solution.py:328
  90.9 5.6 %collective-permute-start.12 = (f32[256,512]{1,0:T(8,128)}, f32[256,512]{1,0:T(8,128)S(1)}, u32[]{:S(2)}, u32[]{:S(2)}) collective-permute-start(f32[256,512]{1,0:T(8,128)} %get-tuple-element.31), channel_id=1, source_target_pairs={{0,5},{1,4},{2,7},{3,6},{4,1},{5,0},{6,3},{7,2},{8,13},{9,12},{10,... | collective-permute-start | bytes 1572872 | tf_op jit(solution)/shard_map/ppermute | solution.py:228
  98.1 42.3 %collective-permute-done.5 = f32[1,2048]{1,0:T(1,128)S(1)} collective-permute-done((f32[1,2048]{1,0:T(1,128)S(1)}, f32[1,2048]{1,0:T(1,128)S(1)}, u32[]{:S(2)}, u32[]{:S(2)}) %collective-permute-start.5) | collective-permute-done | bytes 8224 | tf_op jit(solution)/shard_map/ppermute | solution.py:228
  154.1 30.5 %collective-permute-done.18.refs_4_ = f32[256,512]{1,0:T(8,128)S(1)} collective-permute-done((f32[256,512]{1,0:T(8,128)S(1)}, f32[256,512]{1,0:T(8,128)S(1)}, u32[]{:S(2)}, u32[]{:S(2)}) %collective-permute-start.18) | collective-permute-done | bytes 524320 | tf_op jit(solution)/shard_map/ppermute | solution.py:228
  188.8 13.7 %cauchy.7 = (bf16[4096,1024]{1,0:T(8,128)(2,1)}, bf16[4096,1024]{1,0:T(8,128)(2,1)}) custom-call(s32[9]{0:T(128)} %get-tuple-element.76.place_ref, f32[4096,3]{1,0:T(8,128)} %copy.33.column_ref, f32[4,4096]{1,0:T(4,128)} %pad_maximum_fusion.2.row_ref), custom_call_target="tpu_custom_call" | custom-call | flops 83886080 | bytes 16777216 | tf_op jit(solution)/shard_map/cauchy/pallas_call | solution.py:399
  202.6 13.6 %cauchy.6 = (bf16[4096,1024]{1,0:T(8,128)(2,1)}, bf16[4096,1024]{1,0:T(8,128)(2,1)}) custom-call(s32[9]{0:T(128)} %get-tuple-element.78.place_ref, f32[4096,3]{1,0:T(8,128)} %copy.33.column_ref, f32[4,4096]{1,0:T(4,128)} %pad_maximum_fusion.2.row_ref), custom_call_target="tpu_custom_call" | custom-call | flops 83886080 | bytes 16777216 | tf_op jit(solution)/shard_map/cauchy/pallas_call | solution.py:399
  216.2 13.6 %cauchy.5 = (bf16[4096,1024]{1,0:T(8,128)(2,1)}, bf16[4096,1024]{1,0:T(8,128)(2,1)}) custom-call(s32[9]{0:T(128)} %get-tuple-element.77.place_ref, f32[4096,3]{1,0:T(8,128)} %copy.33.column_ref, f32[4,4096]{1,0:T(4,128)} %pad_maximum_fusion.2.row_ref), custom_call_target="tpu_custom_call" | custom-call | flops 83886080 | bytes 16777216 | tf_op jit(solution)/shard_map/cauchy/pallas_call | solution.py:399
  229.8 13.5 %cauchy.4 = (bf16[4096,1024]{1,0:T(8,128)(2,1)}, bf16[4096,1024]{1,0:T(8,128)(2,1)}) custom-call(s32[9]{0:T(128)} %get-tuple-element.79.place_ref, f32[4096,3]{1,0:T(8,128)} %copy.33.column_ref, f32[4,4096]{1,0:T(4,128)} %pad_maximum_fusion.2.row_ref), custom_call_target="tpu_custom_call" | custom-call | flops 83886080 | bytes 16777216 | tf_op jit(solution)/shard_map/cauchy/pallas_call | solution.py:399
  249.9 13.5 %product.11 = f32[256,1024]{1,0:T(8,128)} custom-call(s32[8]{0:T(128)} %copy-done.6, f32[256,512]{1,0:T(8,128)} %copy-done.2, f32[256,512]{1,0:T(8,128)} %collective-permute-done.8.refs_1_, f32[256,512]{1,0:T(8,128)} %collective-permute-done.9.refs_2_, f32[256,512]{1,0:T(8,128)} %collective-permute-done.10.refs_3_, ...), custom_call_target="tpu_custom_call" | custom-call | flops 6442450944 | bytes 16777216 | tf_op jit(solution)/shard_map/product/pallas_call | solution.py:424
  268.7 14.1 %collective-permute-done.19.refs_5_ = f32[256,512]{1,0:T(8,128)S(1)} collective-permute-done((f32[256,512]{1,0:T(8,128)}, f32[256,512]{1,0:T(8,128)S(1)}, u32[]{:S(2)}, u32[]{:S(2)}) %collective-permute-start.19) | collective-permute-done | bytes 524320 | tf_op jit(solution)/shard_map/ppermute | solution.py:228
  282.8 10.0 %collective-permute-done.15.refs_1_ = f32[256,512]{1,0:T(8,128)S(1)} collective-permute-done((f32[256,512]{1,0:T(8,128)}, f32[256,512]{1,0:T(8,128)S(1)}, u32[]{:S(2)}, u32[]{:S(2)}) %collective-permute-start.15) | collective-permute-done | bytes 524320 | tf_op jit(solution)/shard_map/ppermute | solution.py:228
  296.5 13.4 %product.15 = f32[256,1024]{1,0:T(8,128)} custom-call(s32[8]{0:T(128)} %copy-done.6, f32[256,512]{1,0:T(8,128)} %copy-done.1, f32[256,512]{1,0:T(8,128)} %copy-done.12, f32[256,512]{1,0:T(8,128)} %copy-done.10, f32[256,512]{1,0:T(8,128)} %collective-permute-done.17.refs_3_, f32[256,512]{1,0:T(8,128)} %copy-done.9, f32[256,512]{1,0:T(8,128)} %copy-done.11, ...), custom_call_target="tpu_custom_call" | custom-call | flops 6442450944 | bytes 16777216 | tf_op jit(solution)/shard_map/product/pallas_call | solution.py:424
  310.0 6.1 %collective-permute-start.26 = (f32[256,1024]{1,0:T(8,128)}, f32[256,1024]{1,0:T(8,128)S(1)}, u32[]{:S(2)}, u32[]{:S(2)}) collective-permute-start(f32[256,1024]{1,0:T(8,128)} %product.15), channel_id=1, source_target_pairs={{0,2},{1,3},{2,0},{3,1},{4,6},{5,7},{6,4},{7,5},{8,10},{9,11},{10,... | collective-permute-start | bytes 3145736 | tf_op jit(solution)/shard_map/ppermute | solution.py:228
  316.0 13.4 %product.10 = f32[256,1024]{1,0:T(8,128)} custom-call(s32[8]{0:T(128)} %copy-done.6, f32[256,512]{1,0:T(8,128)} %copy-done.2, f32[256,512]{1,0:T(8,128)} %collective-permute-done.8.refs_1_, f32[256,512]{1,0:T(8,128)} %collective-permute-done.9.refs_2_, f32[256,512]{1,0:T(8,128)} %collective-permute-done.10.refs_3_, ...), custom_call_target="tpu_custom_call" | custom-call | flops 6442450944 | bytes 16777216 | tf_op jit(solution)/shard_map/product/pallas_call | solution.py:424
  329.8 13.5 %product.12 = f32[256,1024]{1,0:T(8,128)} custom-call(s32[8]{0:T(128)} %copy-done.6, f32[256,512]{1,0:T(8,128)} %copy-done.2, f32[256,512]{1,0:T(8,128)} %collective-permute-done.8.refs_1_, f32[256,512]{1,0:T(8,128)} %collective-permute-done.9.refs_2_, f32[256,512]{1,0:T(8,128)} %collective-permute-done.10.refs_3_, ...), custom_call_target="tpu_custom_call" | custom-call | flops 6442450944 | bytes 16777216 | tf_op jit(solution)/shard_map/product/pallas_call | solution.py:424
  344.4 13.5 %product.9 = f32[256,1024]{1,0:T(8,128)} custom-call(s32[8]{0:T(128)} %copy-done.6, f32[256,512]{1,0:T(8,128)} %copy-done.1, f32[256,512]{1,0:T(8,128)} %copy-done.12, f32[256,512]{1,0:T(8,128)} %copy-done.10, f32[256,512]{1,0:T(8,128)} %collective-permute-done.17.refs_3_, f32[256,512]{1,0:T(8,128)} %copy-done.9, f32[256,512]{1,0:T(8,128)} %copy-done.11, ...), custom_call_target="tpu_custom_call" | custom-call | flops 6442450944 | bytes 16777216 | tf_op jit(solution)/shard_map/product/pallas_call | solution.py:424
  358.7 13.4 %product.14 = f32[256,1024]{1,0:T(8,128)} custom-call(s32[8]{0:T(128)} %copy-done.6, f32[256,512]{1,0:T(8,128)} %copy-done.1, f32[256,512]{1,0:T(8,128)} %copy-done.12, f32[256,512]{1,0:T(8,128)} %copy-done.10, f32[256,512]{1,0:T(8,128)} %collective-permute-done.17.refs_3_, f32[256,512]{1,0:T(8,128)} %copy-done.9, f32[256,512]{1,0:T(8,128)} %copy-done.11, ...), custom_call_target="tpu_custom_call" | custom-call | flops 6442450944 | bytes 16777216 | tf_op jit(solution)/shard_map/product/pallas_call | solution.py:424
  372.2 13.4 %product.8 = f32[256,1024]{1,0:T(8,128)} custom-call(s32[8]{0:T(128)} %copy-done.6, f32[256,512]{1,0:T(8,128)} %copy-done.2, f32[256,512]{1,0:T(8,128)} %collective-permute-done.8.refs_1_, f32[256,512]{1,0:T(8,128)} %collective-permute-done.9.refs_2_, f32[256,512]{1,0:T(8,128)} %collective-permute-done.10.refs_3_, ...), custom_call_target="tpu_custom_call" | custom-call | flops 6442450944 | bytes 16777216 | tf_op jit(solution)/shard_map/product/pallas_call | solution.py:424
  391.2 6.8 %all-gather.1 = f32[1024,1]{1,0:T(8,128)S(1)} all-gather(f32[256,1]{1,0:T(8,128)} %norms.1), channel_id=3, replica_groups=mesh['row'=4,'col'=8] {'row'}, dimensions={0}, use_global_device_ids=true | all-gather | bytes 5120 | tf_op jit(solution)/shard_map/all_gather | solution.py:460
  403.8 13.4 %product.13 = f32[256,1024]{1,0:T(8,128)} custom-call(s32[8]{0:T(128)} %copy-done.6, f32[256,512]{1,0:T(8,128)} %copy-done.1, f32[256,512]{1,0:T(8,128)} %copy-done.12, f32[256,512]{1,0:T(8,128)} %copy-done.10, f32[256,512]{1,0:T(8,128)} %collective-permute-done.17.refs_3_, f32[256,512]{1,0:T(8,128)} %copy-done.9, f32[256,512]{1,0:T(8,128)} %copy-done.11, ...), custom_call_target="tpu_custom_call" | custom-call | flops 6442450944 | bytes 16777216 | tf_op jit(solution)/shard_map/product/pallas_call | solution.py:424
  427.9 15.9 %collective-permute-done.25 = f32[256,1024]{1,0:T(8,128)S(1)} collective-permute-done((f32[256,1024]{1,0:T(8,128)}, f32[256,1024]{1,0:T(8,128)S(1)}, u32[]{:S(2)}, u32[]{:S(2)}) %collective-permute-start.25) | collective-permute-done | bytes 1048608 | tf_op jit(solution)/shard_map/ppermute | solution.py:228
  (131 shorter events, 105.0 us)
Async XLA Ops:
  9.2 17.1 %collective-permute-start = (f32[2,512]{1,0:T(2,128)S(1)}, f32[2,512]{1,0:T(2,128)S(1)}, u32[]{:S(2)}, u32[]{:S(2)}) collective-permute-start(f32[2,512]{1,0:T(2,128)S(1)} %psum.7), channel_id=1, source_target_pairs={{0,1},{1,0},{2,3},{3,2},{4,5},{5,4},{6,7},{7,6},{8,9},{9,8},{10,11... | collective-permute-start | bytes 12296 | tf_op jit(solution)/shard_map/ppermute | solution.py:228
  14.6 136.0 %collective-permute-start.11 = (f32[256,512]{1,0:T(8,128)S(1)}, f32[256,512]{1,0:T(8,128)}, u32[]{:S(2)}, u32[]{:S(2)}) collective-permute-start(f32[256,512]{1,0:T(8,128)S(1)} %get-tuple-element.59.refs_0_), channel_id=1, source_target_pairs={{0,4},{1,5},{2,6},{3,7},{4,0},{5,1},{6,2},{7,3},{8,12},{9,13},{10,... | collective-permute-start | bytes 1572872 | tf_op jit(solution)/shard_map/ppermute | solution.py:228
  72.6 12.0 %collective-permute-start.6 = (f32[1,1024]{1,0:T(1,128)S(1)}, f32[1,1024]{1,0:T(1,128)S(1)}, u32[]{:S(2)}, u32[]{:S(2)}) collective-permute-start(f32[1,1024]{1,0:T(1,128)S(1)} %bitcast.38), channel_id=1, source_target_pairs={{0,1},{1,0},{2,3},{3,2},{4,5},{5,4},{6,7},{7,6},{8,9},{9,8},{10,11... | collective-permute-start | bytes 12296 | tf_op jit(solution)/shard_map/ppermute | solution.py:228
  84.6 13.5 %collective-permute-start.7 = (f32[1,2048]{1,0:T(1,128)S(1)}, f32[1,2048]{1,0:T(1,128)S(1)}, u32[]{:S(2)}, u32[]{:S(2)}) collective-permute-start(f32[1,2048]{1,0:T(1,128)S(1)} %pad_maximum_fusion.7), channel_id=1, source_target_pairs={{0,2},{1,3},{2,0},{3,1},{4,6},{5,7},{6,4},{7,5},{8,10},{9,11},{10,... | collective-permute-start | bytes 24584 | tf_op jit(solution)/shard_map/ppermute | solution.py:228
  90.9 60.5 %collective-permute-start.12 = (f32[256,512]{1,0:T(8,128)}, f32[256,512]{1,0:T(8,128)S(1)}, u32[]{:S(2)}, u32[]{:S(2)}) collective-permute-start(f32[256,512]{1,0:T(8,128)} %get-tuple-element.31), channel_id=1, source_target_pairs={{0,5},{1,4},{2,7},{3,6},{4,1},{5,0},{6,3},{7,2},{8,13},{9,12},{10,... | collective-permute-start | bytes 1572872 | tf_op jit(solution)/shard_map/ppermute | solution.py:228
  96.5 56.3 %collective-permute-start.13 = (f32[256,512]{1,0:T(8,128)}, f32[256,512]{1,0:T(8,128)S(1)}, u32[]{:S(2)}, u32[]{:S(2)}) collective-permute-start(f32[256,512]{1,0:T(8,128)} %get-tuple-element.32), channel_id=1, source_target_pairs={{0,6},{1,7},{2,4},{3,5},{4,2},{5,3},{6,0},{7,1},{8,14},{9,15},{10,... | collective-permute-start | bytes 1572872 | tf_op jit(solution)/shard_map/ppermute | solution.py:228
  96.6 43.8 %collective-permute-start.5 = (f32[1,2048]{1,0:T(1,128)S(1)}, f32[1,2048]{1,0:T(1,128)S(1)}, u32[]{:S(2)}, u32[]{:S(2)}) collective-permute-start(f32[1,2048]{1,0:T(1,128)S(1)} %add.118), channel_id=1, source_target_pairs={{0,4},{1,5},{2,6},{3,7},{4,0},{5,1},{6,2},{7,3},{8,12},{9,13},{10,... | collective-permute-start | bytes 24584 | tf_op jit(solution)/shard_map/ppermute | solution.py:228
  146.3 38.2 %collective-permute-start.18 = (f32[256,512]{1,0:T(8,128)S(1)}, f32[256,512]{1,0:T(8,128)S(1)}, u32[]{:S(2)}, u32[]{:S(2)}) collective-permute-start(f32[256,512]{1,0:T(8,128)S(1)} %get-tuple-element.39.refs_0_), channel_id=1, source_target_pairs={{0,4},{1,5},{2,6},{3,7},{4,0},{5,1},{6,2},{7,3},{8,12},{9,13},{10,... | collective-permute-start | bytes 1572872 | tf_op jit(solution)/shard_map/ppermute | solution.py:228
  147.0 101.4 %collective-permute-start.14 = (f32[256,512]{1,0:T(8,128)S(1)}, f32[256,512]{1,0:T(8,128)}, u32[]{:S(2)}, u32[]{:S(2)}) collective-permute-start(f32[256,512]{1,0:T(8,128)S(1)} %get-tuple-element.30), channel_id=1, source_target_pairs={{0,7},{1,6},{2,5},{3,4},{4,3},{5,2},{6,1},{7,0},{8,15},{9,14},{10,... | collective-permute-start | bytes 1572872 | tf_op jit(solution)/shard_map/ppermute | solution.py:228
  150.6 99.3 %collective-permute-start.10 = (f32[256,512]{1,0:T(8,128)S(1)}, f32[256,512]{1,0:T(8,128)}, u32[]{:S(2)}, u32[]{:S(2)}) collective-permute-start(f32[256,512]{1,0:T(8,128)S(1)} %get-tuple-element.30), channel_id=1, source_target_pairs={{0,3},{1,2},{2,1},{3,0},{4,7},{5,6},{6,5},{7,4},{8,11},{9,10},{10,... | collective-permute-start | bytes 1572872 | tf_op jit(solution)/shard_map/ppermute | solution.py:228
  151.4 91.9 %collective-permute-start.8 = (f32[256,512]{1,0:T(8,128)}, f32[256,512]{1,0:T(8,128)}, u32[]{:S(2)}, u32[]{:S(2)}) collective-permute-start(f32[256,512]{1,0:T(8,128)} %get-tuple-element.31), channel_id=1, source_target_pairs={{0,1},{1,0},{2,3},{3,2},{4,5},{5,4},{6,7},{7,6},{8,9},{9,8},{10,11... | collective-permute-start | bytes 1572872 | tf_op jit(solution)/shard_map/ppermute | solution.py:228
  152.9 90.5 %collective-permute-start.9 = (f32[256,512]{1,0:T(8,128)}, f32[256,512]{1,0:T(8,128)}, u32[]{:S(2)}, u32[]{:S(2)}) collective-permute-start(f32[256,512]{1,0:T(8,128)} %get-tuple-element.32), channel_id=1, source_target_pairs={{0,2},{1,3},{2,0},{3,1},{4,6},{5,7},{6,4},{7,5},{8,10},{9,11},{10,... | collective-permute-start | bytes 1572872 | tf_op jit(solution)/shard_map/ppermute | solution.py:228
  184.6 62.8 %collective-permute-start.20 = (f32[256,512]{1,0:T(8,128)S(1)}, f32[256,512]{1,0:T(8,128)}, u32[]{:S(2)}, u32[]{:S(2)}) collective-permute-start(f32[256,512]{1,0:T(8,128)S(1)} %get-tuple-element.37), channel_id=1, source_target_pairs={{0,6},{1,7},{2,4},{3,5},{4,2},{5,3},{6,0},{7,1},{8,14},{9,15},{10,... | collective-permute-start | bytes 1572872 | tf_op jit(solution)/shard_map/ppermute | solution.py:228
  243.3 25.4 %collective-permute-start.16 = (f32[256,512]{1,0:T(8,128)S(1)}, f32[256,512]{1,0:T(8,128)S(1)}, u32[]{:S(2)}, u32[]{:S(2)}) collective-permute-start(f32[256,512]{1,0:T(8,128)S(1)} %get-tuple-element.37), channel_id=1, source_target_pairs={{0,2},{1,3},{2,0},{3,1},{4,6},{5,7},{6,4},{7,5},{8,10},{9,11},{10,... | collective-permute-start | bytes 1572872 | tf_op jit(solution)/shard_map/ppermute | solution.py:228
  243.3 39.5 %collective-permute-start.19 = (f32[256,512]{1,0:T(8,128)}, f32[256,512]{1,0:T(8,128)S(1)}, u32[]{:S(2)}, u32[]{:S(2)}) collective-permute-start(f32[256,512]{1,0:T(8,128)} %get-tuple-element.36), channel_id=1, source_target_pairs={{0,5},{1,4},{2,7},{3,6},{4,1},{5,0},{6,3},{7,2},{8,13},{9,12},{10,... | collective-permute-start | bytes 1572872 | tf_op jit(solution)/shard_map/ppermute | solution.py:228
  247.3 45.5 %collective-permute-start.15 = (f32[256,512]{1,0:T(8,128)}, f32[256,512]{1,0:T(8,128)S(1)}, u32[]{:S(2)}, u32[]{:S(2)}) collective-permute-start(f32[256,512]{1,0:T(8,128)} %get-tuple-element.36), channel_id=1, source_target_pairs={{0,1},{1,0},{2,3},{3,2},{4,5},{5,4},{6,7},{7,6},{8,9},{9,8},{10,11... | collective-permute-start | bytes 1572872 | tf_op jit(solution)/shard_map/ppermute | solution.py:228
  248.4 44.4 %collective-permute-start.21 = (f32[256,512]{1,0:T(8,128)}, f32[256,512]{1,0:T(8,128)}, u32[]{:S(2)}, u32[]{:S(2)}) collective-permute-start(f32[256,512]{1,0:T(8,128)} %get-tuple-element.38), channel_id=1, source_target_pairs={{0,7},{1,6},{2,5},{3,4},{4,3},{5,2},{6,1},{7,0},{8,15},{9,14},{10,... | collective-permute-start | bytes 1572872 | tf_op jit(solution)/shard_map/ppermute | solution.py:228
  249.9 46.6 %collective-permute-start.17 = (f32[256,512]{1,0:T(8,128)}, f32[256,512]{1,0:T(8,128)}, u32[]{:S(2)}, u32[]{:S(2)}) collective-permute-start(f32[256,512]{1,0:T(8,128)} %get-tuple-element.38), channel_id=1, source_target_pairs={{0,3},{1,2},{2,1},{3,0},{4,7},{5,6},{6,5},{7,4},{8,11},{9,10},{10,... | collective-permute-start | bytes 1572872 | tf_op jit(solution)/shard_map/ppermute | solution.py:228
  268.7 153.4 %collective-permute-start.23 = (f32[256,1024]{1,0:T(8,128)}, f32[256,1024]{1,0:T(8,128)S(1)}, u32[]{:S(2)}, u32[]{:S(2)}) collective-permute-start(f32[256,1024]{1,0:T(8,128)} %product.11), channel_id=1, source_target_pairs={{0,2},{1,3},{2,0},{3,1},{4,6},{5,7},{6,4},{7,5},{8,10},{9,11},{10,... | collective-permute-start | bytes 3145736 | tf_op jit(solution)/shard_map/ppermute | solution.py:228
  310.0 135.0 %collective-permute-start.26 = (f32[256,1024]{1,0:T(8,128)}, f32[256,1024]{1,0:T(8,128)S(1)}, u32[]{:S(2)}, u32[]{:S(2)}) collective-permute-start(f32[256,1024]{1,0:T(8,128)} %product.15), channel_id=1, source_target_pairs={{0,2},{1,3},{2,0},{3,1},{4,6},{5,7},{6,4},{7,5},{8,10},{9,11},{10,... | collective-permute-start | bytes 3145736 | tf_op jit(solution)/shard_map/ppermute | solution.py:228
  329.5 87.7 %collective-permute-start.22 = (f32[256,1024]{1,0:T(8,128)}, f32[256,1024]{1,0:T(8,128)}, u32[]{:S(2)}, u32[]{:S(2)}) collective-permute-start(f32[256,1024]{1,0:T(8,128)} %product.10), channel_id=1, source_target_pairs={{0,3},{1,2},{2,1},{3,0},{4,7},{5,6},{6,5},{7,4},{8,11},{9,10},{10,... | collective-permute-start | bytes 3145736 | tf_op jit(solution)/shard_map/ppermute | solution.py:228
  343.2 80.0 %collective-permute-start.24 = (f32[256,1024]{1,0:T(8,128)}, f32[256,1024]{1,0:T(8,128)}, u32[]{:S(2)}, u32[]{:S(2)}) collective-permute-start(f32[256,1024]{1,0:T(8,128)} %product.12), channel_id=1, source_target_pairs={{0,1},{1,0},{2,3},{3,2},{4,5},{5,4},{6,7},{7,6},{8,9},{9,8},{10,11... | collective-permute-start | bytes 3145736 | tf_op jit(solution)/shard_map/ppermute | solution.py:228
  357.9 88.2 %collective-permute-start.27 = (f32[256,1024]{1,0:T(8,128)}, f32[256,1024]{1,0:T(8,128)}, u32[]{:S(2)}, u32[]{:S(2)}) collective-permute-start(f32[256,1024]{1,0:T(8,128)} %product.9), channel_id=1, source_target_pairs={{0,1},{1,0},{2,3},{3,2},{4,5},{5,4},{6,7},{7,6},{8,9},{9,8},{10,11... | collective-permute-start | bytes 3145736 | tf_op jit(solution)/shard_map/ppermute | solution.py:228
  417.2 26.6 %collective-permute-start.25 = (f32[256,1024]{1,0:T(8,128)}, f32[256,1024]{1,0:T(8,128)S(1)}, u32[]{:S(2)}, u32[]{:S(2)}) collective-permute-start(f32[256,1024]{1,0:T(8,128)} %product.14), channel_id=1, source_target_pairs={{0,3},{1,2},{2,1},{3,0},{4,7},{5,6},{6,5},{7,4},{8,11},{9,10},{10,... | collective-permute-start | bytes 3145736 | tf_op jit(solution)/shard_map/ppermute | solution.py:228
  (17 other events, 868.0 us)
